TPU v7x, 512 devices: a whole 4x4x16 slice. The times are simulated.
512 devices in a mesh: grp: 16 (over z_lo, core), row: 32 (over x, y, z_hi).
Axes of the slice: x: 4, y: 4, z: 16 (z_hi: 2, z_lo: 8; z = z_hi * 8 + z_lo), core: 2. Of those that a mesh axis runs over, the one named last changes fastest.
Arguments:
- signal: bfloat16 [2048, 64, 128], P(('grp', 'row')), may hold values from -6 to 6
- leaf_basis: bfloat16 [2048, 64, 128], P(('grp', 'row')), may hold values from -0.5 to 0.5
- near_blocks: bfloat16 [2048, 3, 128, 128], P(('grp', 'row')), may hold values from -0.3125 to 0.3125
- coupling: bfloat16 [98304, 4096], P(('grp', 'row')), may hold values from -0.109375 to 0.109375
- block_cols: int32 [98304], P(('grp', 'row')), may hold values from 0 to 2047, as said below
- block_rows: int32 [98304], P(('grp', 'row')), may hold values from 0 to 3
- block_live: int32 [98304], P(('grp', 'row')), may hold values 0 or 1
Outputs:
- product: bfloat16 [2048, 64, 128], P(('grp', 'row'))
Inputs may be any that keep to these rules, and one draw needn't show every extreme that they name: `block_cols`: slot b of device d (d = b // 192, in group h = d // 32) names a column cluster of group (h + o) mod (16), where o = (b mod 192) // 64 - 1; a group's clusters are g * 128 to (g + 1) * 128 - 1.
All inputs are finite; a program needn't handle non-finite values. No bound on the sum of `block_live` on one device may be relied on, other than what follows from the above.
Results may differ from a plain program's by a relative error of at most 0.0039.
Values may be sent and summed in bfloat16 or wider, within the bound.
A program may use at most 64 MiB of HBM per device.

v0:
```python
import jax
import jax.numpy as jnp
from jax import lax
from jax.sharding import PartitionSpec as P

K = 64
R = 64


def with_halo(block, sides, width, periodic):
    for axis, dim in sides:
        count = lax.axis_size(axis)
        forward = [(i, i + 1) for i in range(count - 1)]
        if periodic:
            forward.append((count - 1, 0))
        backward = [(target, source) for source, target in forward]
        low = lax.ppermute(
            lax.slice_in_dim(block, block.shape[dim] - width, None, axis=dim), axis, forward
        )
        high = lax.ppermute(lax.slice_in_dim(block, 0, width, axis=dim), axis, backward)
        block = jnp.concatenate([low, block, high], axis=dim)
    return block


def per_device(signal, leaf_basis, near_blocks, coupling, block_cols, block_rows, block_live):
    cl_dev = signal.shape[0]
    skeleton = jnp.einsum(
        "crl,ckl->crk", signal, leaf_basis, preferred_element_type=jnp.float32
    ).astype(jnp.bfloat16)
    flat_skel = skeleton.reshape(cl_dev, R * K)
    n_row = lax.axis_size("row")
    n_grp = lax.axis_size("grp")
    group_size = cl_dev * n_row
    panel = lax.all_gather(flat_skel, "row", axis=0, tiled=True)
    window_panel = with_halo(panel, (("grp", 0),), group_size, True)
    my_group = lax.axis_index("grp")
    column_group = block_cols // group_size
    position = (column_group - my_group + 1 + n_grp) % n_grp
    local_ids = position * group_size + block_cols % group_size
    sources = window_panel[local_ids].reshape(-1, R, K)
    sources = sources * block_live.astype(jnp.bfloat16)[:, None, None]
    blocks = coupling.reshape(-1, K, K)
    far_rows = []
    for cluster in range(cl_dev):
        chosen = (block_rows == cluster).astype(jnp.bfloat16)
        masked = sources * chosen[:, None, None]
        far_rows.append(
            jnp.einsum("brm,bkm->rk", masked, blocks, preferred_element_type=jnp.float32)
        )
    far = jnp.stack(far_rows, axis=0)
    far_skeleton = far.astype(jnp.bfloat16)
    total = jnp.einsum("crk,ckl->crl", far_skeleton, leaf_basis, preferred_element_type=jnp.float32)
    padded = with_halo(signal, ((("grp", "row"), 0),), 1, False)
    for index in range(3):
        neighbour = padded[index : index + cl_dev]
        total = total + jnp.einsum(
            "crl,cml->crm", neighbour, near_blocks[:, index], preferred_element_type=jnp.float32
        )
    return total.astype(jnp.bfloat16)


def solution(mesh):
    in_specs = (
        P(("grp", "row"), None, None),
        P(("grp", "row"), None, None),
        P(("grp", "row"), None, None, None),
        P(("grp", "row"), None),
        P(("grp", "row")),
        P(("grp", "row")),
        P(("grp", "row")),
    )
    out_specs = P(("grp", "row"), None, None)
    return jax.shard_map(
        per_device, mesh=mesh, in_specs=in_specs, out_specs=out_specs, check_vma=False
    )
```

profile of v0, /device:TPU:2, one launch (start us, length us, event | category | flops | bytes accessed | tf_op | source)
XLA Modules:
  0.0 215.5 jit_solution(11796397899471478045)
XLA Ops:
  6.6 0.8 copy-done
  7.4 1.0 convolution_convert_fusion
  8.4 0.7 reshape.171
  9.1 117.6 %all-gather.3.cloned.1.call-done = bf16[32,4,4096]{2,1,0:T(4,128)(2,1)} async-done(((bf16[1,4,4096]{2,1,0:T(4,128)(2,1)}), bf16[32,4,4096]{2,1,0:T(4,128)(2,1)}) %all-gather.3.cloned.1.call-update) | async-done | bytes 1048592 | tf_op jit(solution)/shard_map/all_gather | solution.py:34
  126.7 1.3 reshape.172
  128.1 2.1 collective-permute-start
  130.2 10.2 %collective-permute-start.1 = (bf16[128,4096]{1,0:T(8,128)(2,1)S(1)}, bf16[128,4096]{1,0:T(8,128)(2,1)}, u32[]{:S(2)}, u32[]{:S(2)}) collective-permute-start(bf16[128,4096]{1,0:T(8,128)(2,1)S(1)} %reshape.172), channel_id=1, source_target_pairs={{32,0},{64,32},{96,64},{128,96},{160,128},{192,160},{224,192},{256... | collective-permute-start | bytes 3145736 | tf_op jit(solution)/shard_map/ppermute | solution.py:20
  140.4 1.9 collective-permute-start.2
  142.4 15.6 %collective-permute-start.3 = (bf16[1,64,128]{2,1,0:T(8,128)(2,1)S(1)}, bf16[1,64,128]{2,1,0:T(8,128)(2,1)S(1)}, u32[]{:S(2)}, u32[]{:S(2)}) collective-permute-start(bf16[1,64,128]{2,1,0:T(8,128)(2,1)S(1)} %get-tuple-element.9), channel_id=1, source_target_pairs={{1,0},{2,1},{3,2},{4,3},{5,4},{6,5},{7,6},{8,7},{9,8},{10,9},{11,1... | collective-permute-start | bytes 49160 | tf_op jit(solution)/shard_map/ppermute | solution.py:20
  158.1 2.5 %copy.36 = bf16[192,4096]{0,1:T(8,128)(2,1)} copy(bf16[192,4096]{1,0:T(8,128)(2,1)S(1)} %copy-done.4) | data formatting | bytes 3145728 | tf_op args[3]
  160.6 1.1 fusion.75
  161.8 2.0 pad_maximum_fusion
  163.8 2.7 %gather_fusion = bf16[192,4096]{1,0:T(8,128)(2,1)} fusion(bf16[384,4096]{1,0:T(8,128)(2,1)S(1)} %pad_maximum_fusion, s32[1024]{0:T(1024)S(1)} %pad_clamp_fusion), kind=kCustom, calls=%fused_computation | custom fusion | bytes 3146496 | tf_op jit(solution)/shard_map/gather | solution.py:40
  166.5 3.6 %multiply_multiply_fusion.3 = (bf16[192,4096]{1,0:T(8,128)(2,1)}, bf16[192,4096]{1,0:T(8,128)(2,1)}, bf16[192,4096]{1,0:T(8,128)(2,1)S(1)}, bf16[192,4096]{1,0:T(8,128)(2,1)S(1)}) fusion(bf16[192,4096]{1,0:T(8,128)(2,1)} %gather_fusion, bf16[192]{0:T(256)(128)(2,1)S(1)} %get-tuple-element.11, bf16[192]{0:T(256)(128)(2,1)S(1)} %convert_element_type.23, ...), kind=kLoop, calls=%fused_computation.34 | loop fusion | flops 3932160 | bytes 7866240 | tf_op jit(solution)/shard_map/mul | solution.py:46
  170.0 3.8 %copy.35 = bf16[192,4096]{0,1:T(8,128)(2,1)} copy(bf16[192,4096]{1,0:T(8,128)(2,1)} %get-tuple-element.5) | data formatting | bytes 3145728 | tf_op jit(solution)/shard_map/mul | solution.py:46
  173.9 3.8 %copy.39 = bf16[192,4096]{0,1:T(8,128)(2,1)} copy(bf16[192,4096]{1,0:T(8,128)(2,1)} %get-tuple-element.6) | data formatting | bytes 3145728 | tf_op jit(solution)/shard_map/mul | solution.py:46
  177.7 6.8 %fusion.54 = bf16[1,64,64]{2,1,0:T(8,128)(2,1)S(1)} fusion(bf16[192,64,64]{0,2,1:T(8,128)(2,1)} %bitcast.56, bf16[192,64,64]{0,2,1:T(8,128)(2,1)} %bitcast.60), kind=kOutput, calls=%fused_computation.27 | convolution fusion | flops 100667392 | bytes 3153920 | tf_op jit(solution)/shard_map/brm,bkm->rk/dot_general | solution.py:48
  184.6 4.4 %fusion.59 = bf16[1,64,64]{2,1,0:T(8,128)(2,1)S(1)} fusion(bf16[192,64,64]{0,2,1:T(8,128)(2,1)S(1)} %bitcast.59, bf16[192,64,64]{0,2,1:T(8,128)(2,1)S(1)} %bitcast.61), kind=kOutput, calls=%fused_computation.28 | convolution fusion | flops 100667392 | bytes 3153920 | tf_op jit(solution)/shard_map/brm,bkm->rk/dot_general | solution.py:48
  189.0 2.6 %copy.42 = bf16[192,4096]{0,1:T(8,128)(2,1)} copy(bf16[192,4096]{1,0:T(8,128)(2,1)S(1)} %get-tuple-element.7) | data formatting | bytes 3145728 | tf_op jit(solution)/shard_map/mul | solution.py:46
  191.6 6.6 %fusion.64 = bf16[1,64,64]{2,1,0:T(8,128)(2,1)S(1)} fusion(bf16[192,64,64]{0,2,1:T(8,128)(2,1)} %bitcast.57, bf16[192,64,64]{0,2,1:T(8,128)(2,1)} %bitcast.63), kind=kOutput, calls=%fused_computation.29 | convolution fusion | flops 100667392 | bytes 3153920 | tf_op jit(solution)/shard_map/brm,bkm->rk/dot_general | solution.py:48
  198.3 2.5 %copy.45 = bf16[192,4096]{0,1:T(8,128)(2,1)} copy(bf16[192,4096]{1,0:T(8,128)(2,1)S(1)} %get-tuple-element.8) | data formatting | bytes 3145728 | tf_op jit(solution)/shard_map/mul | solution.py:46
  200.7 6.7 %fusion.69 = bf16[1,64,64]{2,1,0:T(8,128)(2,1)S(1)} fusion(bf16[192,64,64]{0,2,1:T(8,128)(2,1)} %bitcast.58, bf16[192,64,64]{0,2,1:T(8,128)(2,1)} %bitcast.62), kind=kOutput, calls=%fused_computation.30 | convolution fusion | flops 100667392 | bytes 3153920 | tf_op jit(solution)/shard_map/brm,bkm->rk/dot_general | solution.py:48
  207.6 0.2 fusion.12
  207.8 0.8 fusion.13
  (31 shorter events, 0.3 us)
Async XLA Ops:
  6.5 0.8 copy-start
  6.5 133.9 %copy-start.5 = (bf16[4,64,128]{2,1,0:T(8,128)(2,1)S(1)}, bf16[4,64,128]{2,1,0:T(8,128)(2,1)}, u32[]{:S(2)}) copy-start(bf16[4,64,128]{2,1,0:T(8,128)(2,1)} %param.7) | copy-start | bytes 196612
  6.5 151.5 %copy-start.9 = (s32[192]{0:T(256)S(1)}, s32[192]{0:T(256)}, u32[]{:S(2)}) copy-start(s32[192]{0:T(256)} %param.13) | copy-start | bytes 2308
  6.5 151.5 %copy-start.4 = (bf16[192,4096]{1,0:T(8,128)(2,1)S(1)}, bf16[192,4096]{1,0:T(8,128)(2,1)}, u32[]{:S(2)}) copy-start(bf16[192,4096]{1,0:T(8,128)(2,1)} %param.10) | copy-start | bytes 4718596
  6.5 120.2 %all-gather.3.cloned.1.call-start = ((), (), s32[]{:S(2)}) async-start(), calls=%async_computation | async-start | bytes 1081344 | tf_op jit(solution)/shard_map/all_gather | solution.py:34
  128.1 33.7 %copy-start.1 = (bf16[128,4096]{1,0:T(8,128)(2,1)}, bf16[128,4096]{1,0:T(8,128)(2,1)S(1)}, u32[]{:S(2)}) copy-start(bf16[128,4096]{1,0:T(8,128)(2,1)S(1)} %reshape.172) | copy-start | bytes 3145732
  128.1 32.5 %copy-start.8 = (s32[192]{0:T(256)S(1)}, s32[192]{0:T(256)}, u32[]{:S(2)}) copy-start(s32[192]{0:T(256)} %param.11) | copy-start | bytes 2308
  128.1 32.5 %copy-start.7 = (s32[192]{0:T(256)S(1)}, s32[192]{0:T(256)}, u32[]{:S(2)}) copy-start(s32[192]{0:T(256)} %param.12) | copy-start | bytes 2308
  128.1 33.6 %collective-permute-start = (bf16[128,4096]{1,0:T(8,128)(2,1)S(1)}, bf16[128,4096]{1,0:T(8,128)(2,1)}, u32[]{:S(2)}, u32[]{:S(2)}) collective-permute-start(bf16[128,4096]{1,0:T(8,128)(2,1)S(1)} %reshape.172), channel_id=1, source_target_pairs={{0,32},{32,64},{64,96},{96,128},{128,160},{160,192},{192,224},{224... | collective-permute-start | bytes 3145736 | tf_op jit(solution)/shard_map/ppermute | solution.py:17
  130.2 31.6 %collective-permute-start.1 = (bf16[128,4096]{1,0:T(8,128)(2,1)S(1)}, bf16[128,4096]{1,0:T(8,128)(2,1)}, u32[]{:S(2)}, u32[]{:S(2)}) collective-permute-start(bf16[128,4096]{1,0:T(8,128)(2,1)S(1)} %reshape.172), channel_id=1, source_target_pairs={{32,0},{64,32},{96,64},{128,96},{160,128},{192,160},{224,192},{256... | collective-permute-start | bytes 3145736 | tf_op jit(solution)/shard_map/ppermute | solution.py:20
  140.4 67.1 %collective-permute-start.2 = (bf16[1,64,128]{2,1,0:T(8,128)(2,1)S(1)}, bf16[1,64,128]{2,1,0:T(8,128)(2,1)S(1)}, u32[]{:S(2)}, u32[]{:S(2)}) collective-permute-start(bf16[1,64,128]{2,1,0:T(8,128)(2,1)S(1)} %get-tuple-element.10), channel_id=1, source_target_pairs={{0,1},{1,2},{2,3},{3,4},{4,5},{5,6},{6,7},{7,8},{8,9},{9,10},{10,1... | collective-permute-start | bytes 49160 | tf_op jit(solution)/shard_map/ppermute | solution.py:17
  142.4 65.4 %collective-permute-start.3 = (bf16[1,64,128]{2,1,0:T(8,128)(2,1)S(1)}, bf16[1,64,128]{2,1,0:T(8,128)(2,1)S(1)}, u32[]{:S(2)}, u32[]{:S(2)}) collective-permute-start(bf16[1,64,128]{2,1,0:T(8,128)(2,1)S(1)} %get-tuple-element.9), channel_id=1, source_target_pairs={{1,0},{2,1},{3,2},{4,3},{5,4},{6,5},{7,6},{8,7},{9,8},{10,9},{11,1... | collective-permute-start | bytes 49160 | tf_op jit(solution)/shard_map/ppermute | solution.py:20
  177.7 6.8 %copy-start.2 = (bf16[192,4096]{0,1:T(8,128)(2,1)S(1)}, bf16[192,4096]{0,1:T(8,128)(2,1)}, u32[]{:S(2)}) copy-start(bf16[192,4096]{0,1:T(8,128)(2,1)} %copy.36) | copy-start | bytes 4718596
  177.7 6.8 %copy-start.3 = (bf16[192,4096]{0,1:T(8,128)(2,1)S(1)}, bf16[192,4096]{0,1:T(8,128)(2,1)}, u32[]{:S(2)}) copy-start(bf16[192,4096]{0,1:T(8,128)(2,1)} %copy.39) | copy-start | bytes 4718596
  200.7 6.9 %copy-start.6 = (bf16[4,3,128,128]{3,2,1,0:T(8,128)(2,1)S(1)}, bf16[4,3,128,128]{3,2,1,0:T(8,128)(2,1)}, u32[]{:S(2)}) copy-start(bf16[4,3,128,128]{3,2,1,0:T(8,128)(2,1)} %param.9) | copy-start | bytes 1179652
Sparse Core Ops, SparseCore 0:
  11.7 115.0 all-gather.2
where the time goes:
time: 216 us; the launch traced here: 215 us
  waiting for transfers between devices  118 us (55%)
  starting transfers between devices  29.9 us (14%)
  matrix products  27.8 us (13%)
  local copies, waits for them, and re-layouts  20.9 us (10%)
  between operations  13.7 us (6%)
  other arithmetic  5.57 us (3%)
    all_gather x1, waiting for transfers between devices, per_device(): panel = lax.all_gather(flat_skel, 'row', axis=0, tiled=True)  118 us
    ppermute x2, starting transfers between devices, with_halo(): lax.ppermute(lax.slice_in_dim(block, 0, width, axis=dim), axis, backward)  25.9 us
    dot_general x4, matrix products, per_device(): jnp.einsum('brm,bkm->rk', masked, blocks, preferred_element_type=jnp.floa...  24.6 us
    mul x4, local copies, waits for them, and re-layouts, per_device(): masked = sources * chosen[:, None, None]  12.8 us
    unnamed x23, local copies, waits for them, and re-layouts  5.42 us
  transfers between devices with their start and end apart: 5, of which 1 were waited for; matrix products, arithmetic and copies ran while one was open for 23% of the time, Pallas kernels for 0%

commit v1 on v0

--- a/solution.py
+++ b/solution.py
@@ -31,7 +31,9 @@
     n_row = lax.axis_size("row")
     n_grp = lax.axis_size("grp")
     group_size = cl_dev * n_row
-    panel = lax.all_gather(flat_skel, "row", axis=0, tiled=True)
+    panel = jnp.concatenate(
+        lax.all_to_all(jnp.stack([flat_skel] * lax.axis_size("row")), "row", 0, 0), axis=0
+    )
     window_panel = with_halo(panel, (("grp", 0),), group_size, True)
     my_group = lax.axis_index("grp")
     column_group = block_cols // group_size

time: 216 us -> 162 us (0.75)
  the two profiles are of different devices: /device:TPU:2 before, /device:TPU:1 now
where the time goes in v1:
time: 162 us; the launch traced here: 161 us
  starting transfers between devices  53.6 us (33%)
  blocking collectives  51.9 us (32%)
  matrix products  27.8 us (17%)
  local copies, waits for them, and re-layouts  22.1 us (14%)
  other arithmetic  5.55 us (3%)
    all_to_all x1, blocking collectives, per_device(): lax.all_to_all(jnp.stack([flat_skel] * lax.axis_size('row')), 'row', 0, 0)  51.9 us
    ppermute x2, starting transfers between devices, with_halo(): lax.ppermute(lax.slice_in_dim(block, block.shape[dim] - width, None, axis...  35.3 us
    dot_general x4, matrix products, per_device(): jnp.einsum('brm,bkm->rk', masked, blocks, preferred_element_type=jnp.floa...  24.6 us
    ppermute x2, starting transfers between devices, with_halo(): lax.ppermute(lax.slice_in_dim(block, 0, width, axis=dim), axis, backward)  18.3 us
    mul x4, local copies, waits for them, and re-layouts, per_device(): masked = sources * chosen[:, None, None]  12.8 us
    unnamed x21, local copies, waits for them, and re-layouts  5.72 us
    mul x1, other arithmetic, per_device(): masked = sources * chosen[:, None, None]  3.54 us
  transfers between devices with their start and end apart: 4, of which 0 were waited for; matrix products, arithmetic and copies ran while one was open for 32% of the time, Pallas kernels for 0%

profile of v1, /device:TPU:1, one launch (start us, length us, event | category | flops | bytes accessed | tf_op | source)
XLA Modules:
  0.0 161.3 jit_solution(15960940029960990189)
XLA Ops:
  0.0 0.8 copy-done
  0.8 1.0 convolution_convert_fusion
  2.0 0.5 stack.23
  2.5 51.9 %all_to_all.5 = bf16[32,4,4096]{2,1,0:T(4,128)(2,1)S(1)} all-to-all(bf16[32,4,4096]{2,1,0:T(4,128)(2,1)S(1)} %stack.23), channel_id=1, replica_groups=mesh['grp'=16,'row'=32] {'row'}, dimensions={0} | all-to-all | bytes 2097152 | tf_op jit(solution)/shard_map/all_to_all | solution.py:35
  54.4 0.3 reshape.162
  54.7 33.2 %collective-permute-start = (bf16[128,4096]{1,0:T(8,128)(2,1)S(1)}, bf16[128,4096]{1,0:T(8,128)(2,1)S(1)}, u32[]{:S(2)}, u32[]{:S(2)}) collective-permute-start(bf16[128,4096]{1,0:T(8,128)(2,1)S(1)} %reshape.162), channel_id=1, source_target_pairs={{0,32},{32,64},{64,96},{96,128},{128,160},{160,192},{192,224},{224... | collective-permute-start | bytes 3145736 | tf_op jit(solution)/shard_map/ppermute | solution.py:17
  87.9 1.9 %collective-permute-start.1 = (bf16[128,4096]{1,0:T(8,128)(2,1)S(1)}, bf16[128,4096]{1,0:T(8,128)(2,1)}, u32[]{:S(2)}, u32[]{:S(2)}) collective-permute-start(bf16[128,4096]{1,0:T(8,128)(2,1)S(1)} %reshape.162), channel_id=1, source_target_pairs={{32,0},{64,32},{96,64},{128,96},{160,128},{192,160},{224,192},{256... | collective-permute-start | bytes 3145736 | tf_op jit(solution)/shard_map/ppermute | solution.py:20
  89.8 2.1 %collective-permute-start.2 = (bf16[1,64,128]{2,1,0:T(8,128)(2,1)S(1)}, bf16[1,64,128]{2,1,0:T(8,128)(2,1)S(1)}, u32[]{:S(2)}, u32[]{:S(2)}) collective-permute-start(bf16[1,64,128]{2,1,0:T(8,128)(2,1)S(1)} %get-tuple-element.10), channel_id=1, source_target_pairs={{0,1},{1,2},{2,3},{3,4},{4,5},{5,6},{6,7},{7,8},{8,9},{9,10},{10,1... | collective-permute-start | bytes 49160 | tf_op jit(solution)/shard_map/ppermute | solution.py:17
  92.0 16.4 %collective-permute-start.3 = (bf16[1,64,128]{2,1,0:T(8,128)(2,1)S(1)}, bf16[1,64,128]{2,1,0:T(8,128)(2,1)S(1)}, u32[]{:S(2)}, u32[]{:S(2)}) collective-permute-start(bf16[1,64,128]{2,1,0:T(8,128)(2,1)S(1)} %get-tuple-element.9), channel_id=1, source_target_pairs={{1,0},{2,1},{3,2},{4,3},{5,4},{6,5},{7,6},{8,7},{9,8},{10,9},{11,1... | collective-permute-start | bytes 49160 | tf_op jit(solution)/shard_map/ppermute | solution.py:20
  108.4 3.9 %copy.20 = bf16[192,4096]{0,1:T(8,128)(2,1)} copy(bf16[192,4096]{1,0:T(8,128)(2,1)} %param.10) | data formatting | bytes 3145728 | tf_op args[3]
  112.3 1.1 fusion.75
  113.4 1.0 copy-done.5
  114.4 2.0 %pad_maximum_fusion = bf16[384,4096]{1,0:T(8,128)(2,1)S(1)} fusion(bf16[128,4096]{1,0:T(8,128)(2,1)} %collective-permute-done.1, bf16[128,4096]{1,0:T(8,128)(2,1)} %copy-done.1, bf16[128,4096]{1,0:T(8,128)(2,1)} %copy-done.5), kind=kLoop, calls=%fused_computation.1 | loop fusion | flops 9437184 | bytes 6291456 | tf_op jit(solution)/shard_map/concatenate | solution.py:21
  116.4 2.7 %gather_fusion = bf16[192,4096]{1,0:T(8,128)(2,1)} fusion(bf16[384,4096]{1,0:T(8,128)(2,1)S(1)} %pad_maximum_fusion, s32[1024]{0:T(1024)S(1)} %pad_clamp_fusion), kind=kCustom, calls=%fused_computation | custom fusion | bytes 3146496 | tf_op jit(solution)/shard_map/gather | solution.py:42
  119.1 3.5 %multiply_multiply_fusion.3 = (bf16[192,4096]{1,0:T(8,128)(2,1)}, bf16[192,4096]{1,0:T(8,128)(2,1)}, bf16[192,4096]{1,0:T(8,128)(2,1)S(1)}, bf16[192,4096]{1,0:T(8,128)(2,1)S(1)}) fusion(bf16[192,4096]{1,0:T(8,128)(2,1)} %gather_fusion, bf16[192]{0:T(256)(128)(2,1)S(1)} %get-tuple-element.11, bf16[192]{0:T(256)(128)(2,1)S(1)} %convert_element_type.23, ...), kind=kLoop, calls=%fused_computation.34 | loop fusion | flops 3932160 | bytes 7866240 | tf_op jit(solution)/shard_map/mul | solution.py:48
  122.6 3.8 %copy.19 = bf16[192,4096]{0,1:T(8,128)(2,1)} copy(bf16[192,4096]{1,0:T(8,128)(2,1)} %get-tuple-element.5) | data formatting | bytes 3145728 | tf_op jit(solution)/shard_map/mul | solution.py:48
  126.5 3.8 %copy.23 = bf16[192,4096]{0,1:T(8,128)(2,1)} copy(bf16[192,4096]{1,0:T(8,128)(2,1)} %get-tuple-element.6) | data formatting | bytes 3145728 | tf_op jit(solution)/shard_map/mul | solution.py:48
  130.3 6.8 %fusion.54 = bf16[1,64,64]{2,1,0:T(8,128)(2,1)S(1)} fusion(bf16[192,64,64]{0,2,1:T(8,128)(2,1)} %bitcast.56, bf16[192,64,64]{0,2,1:T(8,128)(2,1)} %bitcast.60), kind=kOutput, calls=%fused_computation.27 | convolution fusion | flops 100667392 | bytes 3153920 | tf_op jit(solution)/shard_map/brm,bkm->rk/dot_general | solution.py:50
  137.2 4.4 %fusion.59 = bf16[1,64,64]{2,1,0:T(8,128)(2,1)S(1)} fusion(bf16[192,64,64]{0,2,1:T(8,128)(2,1)S(1)} %bitcast.59, bf16[192,64,64]{0,2,1:T(8,128)(2,1)S(1)} %bitcast.61), kind=kOutput, calls=%fused_computation.28 | convolution fusion | flops 100667392 | bytes 3153920 | tf_op jit(solution)/shard_map/brm,bkm->rk/dot_general | solution.py:50
  141.6 2.7 %copy.26 = bf16[192,4096]{0,1:T(8,128)(2,1)} copy(bf16[192,4096]{1,0:T(8,128)(2,1)S(1)} %get-tuple-element.7) | data formatting | bytes 3145728 | tf_op jit(solution)/shard_map/mul | solution.py:48
  144.2 6.6 %fusion.64 = bf16[1,64,64]{2,1,0:T(8,128)(2,1)S(1)} fusion(bf16[192,64,64]{0,2,1:T(8,128)(2,1)} %bitcast.57, bf16[192,64,64]{0,2,1:T(8,128)(2,1)} %bitcast.63), kind=kOutput, calls=%fused_computation.29 | convolution fusion | flops 100667392 | bytes 3153920 | tf_op jit(solution)/shard_map/brm,bkm->rk/dot_general | solution.py:50
  150.9 2.5 %copy.29 = bf16[192,4096]{0,1:T(8,128)(2,1)} copy(bf16[192,4096]{1,0:T(8,128)(2,1)S(1)} %get-tuple-element.8) | data formatting | bytes 3145728 | tf_op jit(solution)/shard_map/mul | solution.py:48
  153.4 6.7 %fusion.69 = bf16[1,64,64]{2,1,0:T(8,128)(2,1)S(1)} fusion(bf16[192,64,64]{0,2,1:T(8,128)(2,1)} %bitcast.58, bf16[192,64,64]{0,2,1:T(8,128)(2,1)} %bitcast.62), kind=kOutput, calls=%fused_computation.30 | convolution fusion | flops 100667392 | bytes 3153920 | tf_op jit(solution)/shard_map/brm,bkm->rk/dot_general | solution.py:50
  160.4 0.8 fusion.13
  (30 shorter events, 0.6 us)
Async XLA Ops:
  0.0 0.8 copy-start
  2.4 87.4 %copy-start.4 = (bf16[4,64,128]{2,1,0:T(8,128)(2,1)S(1)}, bf16[4,64,128]{2,1,0:T(8,128)(2,1)}, u32[]{:S(2)}) copy-start(bf16[4,64,128]{2,1,0:T(8,128)(2,1)} %param.7) | copy-start | bytes 196612
  2.4 105.9 %copy-start.9 = (s32[192]{0:T(256)S(1)}, s32[192]{0:T(256)}, u32[]{:S(2)}) copy-start(s32[192]{0:T(256)} %param.13) | copy-start | bytes 2308
  54.6 58.8 %copy-start.1 = (bf16[128,4096]{1,0:T(8,128)(2,1)}, bf16[128,4096]{1,0:T(8,128)(2,1)S(1)}, u32[]{:S(2)}) copy-start(bf16[128,4096]{1,0:T(8,128)(2,1)S(1)} %reshape.162) | copy-start | bytes 3145732
  54.6 57.6 %copy-start.8 = (s32[192]{0:T(256)S(1)}, s32[192]{0:T(256)}, u32[]{:S(2)}) copy-start(s32[192]{0:T(256)} %param.11) | copy-start | bytes 2308
  54.7 57.6 %copy-start.7 = (s32[192]{0:T(256)S(1)}, s32[192]{0:T(256)}, u32[]{:S(2)}) copy-start(s32[192]{0:T(256)} %param.12) | copy-start | bytes 2308
  54.7 58.7 %collective-permute-start = (bf16[128,4096]{1,0:T(8,128)(2,1)S(1)}, bf16[128,4096]{1,0:T(8,128)(2,1)S(1)}, u32[]{:S(2)}, u32[]{:S(2)}) collective-permute-start(bf16[128,4096]{1,0:T(8,128)(2,1)S(1)} %reshape.162), channel_id=1, source_target_pairs={{0,32},{32,64},{64,96},{96,128},{128,160},{160,192},{192,224},{224... | collective-permute-start | bytes 3145736 | tf_op jit(solution)/shard_map/ppermute | solution.py:17
  87.9 26.5 %collective-permute-start.1 = (bf16[128,4096]{1,0:T(8,128)(2,1)S(1)}, bf16[128,4096]{1,0:T(8,128)(2,1)}, u32[]{:S(2)}, u32[]{:S(2)}) collective-permute-start(bf16[128,4096]{1,0:T(8,128)(2,1)S(1)} %reshape.162), channel_id=1, source_target_pairs={{32,0},{64,32},{96,64},{128,96},{160,128},{192,160},{224,192},{256... | collective-permute-start | bytes 3145736 | tf_op jit(solution)/shard_map/ppermute | solution.py:20
  89.8 70.4 %collective-permute-start.2 = (bf16[1,64,128]{2,1,0:T(8,128)(2,1)S(1)}, bf16[1,64,128]{2,1,0:T(8,128)(2,1)S(1)}, u32[]{:S(2)}, u32[]{:S(2)}) collective-permute-start(bf16[1,64,128]{2,1,0:T(8,128)(2,1)S(1)} %get-tuple-element.10), channel_id=1, source_target_pairs={{0,1},{1,2},{2,3},{3,4},{4,5},{5,6},{6,7},{7,8},{8,9},{9,10},{10,1... | collective-permute-start | bytes 49160 | tf_op jit(solution)/shard_map/ppermute | solution.py:17
  92.0 68.5 %collective-permute-start.3 = (bf16[1,64,128]{2,1,0:T(8,128)(2,1)S(1)}, bf16[1,64,128]{2,1,0:T(8,128)(2,1)S(1)}, u32[]{:S(2)}, u32[]{:S(2)}) collective-permute-start(bf16[1,64,128]{2,1,0:T(8,128)(2,1)S(1)} %get-tuple-element.9), channel_id=1, source_target_pairs={{1,0},{2,1},{3,2},{4,3},{5,4},{6,5},{7,6},{8,7},{9,8},{10,9},{11,1... | collective-permute-start | bytes 49160 | tf_op jit(solution)/shard_map/ppermute | solution.py:20
  113.4 1.0 copy-start.5
  130.3 6.8 %copy-start.2 = (bf16[192,4096]{0,1:T(8,128)(2,1)S(1)}, bf16[192,4096]{0,1:T(8,128)(2,1)}, u32[]{:S(2)}) copy-start(bf16[192,4096]{0,1:T(8,128)(2,1)} %copy.20) | copy-start | bytes 4718596
  130.3 6.8 %copy-start.3 = (bf16[192,4096]{0,1:T(8,128)(2,1)S(1)}, bf16[192,4096]{0,1:T(8,128)(2,1)}, u32[]{:S(2)}) copy-start(bf16[192,4096]{0,1:T(8,128)(2,1)} %copy.23) | copy-start | bytes 4718596
  153.4 6.9 %copy-start.6 = (bf16[4,3,128,128]{3,2,1,0:T(8,128)(2,1)S(1)}, bf16[4,3,128,128]{3,2,1,0:T(8,128)(2,1)}, u32[]{:S(2)}) copy-start(bf16[4,3,128,128]{3,2,1,0:T(8,128)(2,1)} %param.9) | copy-start | bytes 1179652
